TPU v7x, 32 devices: a whole 2x2x4 slice. The times are simulated.
32 devices in a mesh: tm: 2 (over y), space: 16 (over z, x, core).
Axes of the slice: x: 2, y: 2, z: 4, core: 2. Of those that a mesh axis runs over, the one named last changes fastest.
Arguments:
- noisy_state: float32 [8, 2, 256, 256], P('tm', None, 'space'), may hold values from -6 to 6
- fresh_noise: float32 [8, 2, 256, 256], P('tm', None, 'space'), may hold values from -6 to 6
- level_index: int32 [1], replicated, may hold values from 1 to 31
- station_obs: float32 [8, 2, 2048], P('tm', None, 'space'), may hold values from -6 to 6
- obs_variance: float32 [2048], P('space'), may hold values from 0.05 to 0.5
- station_owner: int32 [2048, 1], P('space'), may hold values from 0 to 15; in each aligned block of 128 rows (0 to 127, 128 to 255, ...) at most 32 rows name the same one
- station_cell: int32 [2048], P('space'), may hold values from 0 to 4095
- conv_in: bfloat16 [3, 64, 48], replicated, may hold values from -0.5 to 0.5
- conv_mid: bfloat16 [3, 64, 192], replicated, may hold values from -0.25 to 0.25
- conv_res: bfloat16 [3, 64, 192], replicated, may hold values from -0.25 to 0.25
- conv_out: bfloat16 [3, 16, 192], replicated, may hold values from -0.25 to 0.25
- in_bias: float32 [64], replicated, may hold values from -3 to 3
- noise_embed: float32 [64], replicated, may hold values from -3 to 3
- norm_gain: float32 [64], replicated, may hold values from 0.5 to 2
Outputs:
- next_state: float32 [8, 2, 256, 256], P('tm', None, 'space')
Inputs may be any that keep to these rules, and one draw needn't show every extreme that they name: `station_owner`: among the stations of one device (each aligned block of 128 stations) at most 32 have the same owner strip; every strip owns some station.
All inputs are finite; a program needn't handle non-finite values.
Results may differ from a plain program's by a relative error of at most 0.0023.
Values may be sent and summed in bfloat16 or wider, within the bound.
A program may use at most 64 MiB of HBM per device.

v0:
```python
import jax
import jax.numpy as jnp
from jax import lax
from jax.sharding import PartitionSpec as P

WIN = 8
LEVELS = 32
STRIDE = 4
CHAN = 16


def extended_2(cells, sides, width):
    for axis, dim in sides:
        count = lax.axis_size(axis)
        head = lax.slice_in_dim(cells, 0, width, axis=dim)
        tail = lax.slice_in_dim(cells, cells.shape[dim] - width, cells.shape[dim], axis=dim)
        cells = jnp.concatenate(
            [
                lax.ppermute(tail, axis, [(i, (i + 1) % count) for i in range(count)]),
                cells,
                lax.ppermute(head, axis, [((i + 1) % count, i) for i in range(count)]),
            ],
            axis=dim,
        )
    return cells


def shifted(value, axis, steps):
    count = lax.axis_size(axis)
    first, last = (max(0, -steps), min(count, count - steps))
    return lax.ppermute(value, axis, [(source, source + steps) for source in range(first, last)])


def scale_at(level):
    return 0.3 * jnp.exp(jnp.log(5.0) * level.astype(jnp.float32) / (LEVELS - 1))


def conv_rows(weight, padded):
    out_rows = padded.shape[2] - 2
    stacked = jnp.concatenate(
        [jnp.roll(padded, 1 - col_tap, axis=3) for col_tap in range(3)], axis=1
    )
    total = None
    for row_tap in range(3):
        product = jnp.einsum(
            "oc,ncyx->noyx",
            weight[row_tap],
            stacked[:, :, row_tap : row_tap + out_rows, :],
            preferred_element_type=jnp.float32,
        )
        total = product if total is None else total + product
    return total


def hidden_rim(hidden):
    return extended_2(hidden, (("space", 2),), 1)


def score_net(windows, conv_in, conv_mid, conv_res, conv_out, bias, norm_gain):
    source = extended_2(windows, (("space", 2),), 1)
    first = jax.nn.silu(conv_rows(conv_in, source) + bias[None, :, None, None]).astype(jnp.bfloat16)
    middle = conv_rows(conv_mid, hidden_rim(first))
    normed = (
        middle
        * lax.rsqrt(jnp.mean(middle * middle, axis=1, keepdims=True) + 1e-05)
        * norm_gain[None, :, None, None]
    )
    second = jax.nn.silu(normed).astype(jnp.bfloat16)
    branch = jax.nn.silu(conv_rows(conv_res, hidden_rim(second)))
    third = (first.astype(jnp.float32) + branch).astype(jnp.bfloat16)
    return conv_rows(conv_out, hidden_rim(third))


def local(
    noisy_state,
    fresh_noise,
    level_index,
    station_obs,
    obs_variance,
    station_owner,
    station_cell,
    conv_in,
    conv_mid,
    conv_res,
    conv_out,
    in_bias,
    noise_embed,
    norm_gain,
):
    step_count, layer_count, row_count, col_count = noisy_state.shape
    noise_scale = scale_at(level_index[0])
    next_scale = scale_at(level_index[0] - 1)
    bias = in_bias + noise_embed * jnp.log(10.0 * noise_scale)
    scaled = (noisy_state / jnp.sqrt(1.0 + noise_scale * noise_scale)).astype(jnp.bfloat16)
    time_rank = lax.axis_index("tm")
    total_steps = step_count * lax.axis_size("tm")
    ahead = shifted(scaled, "tm", -1)
    extended = jnp.concatenate([scaled, ahead], axis=0)
    offset = 0
    window_count = (extended.shape[0] - WIN) // STRIDE + 1
    windows = jnp.stack([extended])
    windows = windows.reshape(window_count, CHAN, row_count, col_count)
    outputs = score_net(windows, conv_in, conv_mid, conv_res, conv_out, bias, norm_gain)
    starts = time_rank * step_count - offset + STRIDE * jnp.arange(window_count, dtype=jnp.int32)
    usable = ((starts >= 0) & (starts + WIN <= total_steps)).astype(jnp.float32)
    halves = (
        outputs.reshape(window_count, 2, STRIDE, layer_count, row_count, col_count)
        * usable[:, None, None, None, None, None]
    )
    blank = jnp.zeros((1, STRIDE, layer_count, row_count, col_count), jnp.float32)
    summed = jnp.concatenate([halves[:, 0], blank], axis=0) + jnp.concatenate(
        [blank, halves[:, 1]], axis=0
    )
    summed = summed.reshape(extended.shape[0], layer_count, row_count, col_count)
    spill = shifted(summed[step_count:], "tm", 1)
    own = jnp.concatenate([summed[:STRIDE] + spill, summed[STRIDE:step_count]], axis=0)
    moment = time_rank * step_count + jnp.arange(step_count, dtype=jnp.int32)
    cover = jnp.where((moment < STRIDE) | (moment >= total_steps - STRIDE), 1.0, 2.0).astype(
        jnp.float32
    )
    estimate = noisy_state - noise_scale * (own / cover[:, None, None, None])
    space_size = lax.axis_size("space")
    station_count = station_cell.shape[0]
    capacity = 4 * station_count // space_size
    values = station_obs.reshape(step_count * layer_count, station_count)
    target = station_owner[:, 0]
    earlier = lax.broadcasted_iota(
        jnp.int32, (station_count, station_count), 0
    ) < lax.broadcasted_iota(jnp.int32, (station_count, station_count), 1)
    ranked = jnp.sum(
        jnp.where((target[:, None] == target[None, :]) & earlier, 1, 0), axis=0
    ).astype(jnp.int32)
    slot = target * capacity + ranked
    slot_count = space_size * capacity
    value_slots = jnp.zeros((values.shape[0], slot_count), jnp.float32).at[:, slot].set(values)
    spread_slots = jnp.zeros((1, slot_count), jnp.float32).at[0, slot].set(obs_variance)
    cell_slots = jnp.full((1, slot_count), -1, jnp.int32).at[0, slot].set(station_cell)
    got_values, got_spread, got_cells = (
        lax.all_to_all(value_slots, "space", split_axis=1, concat_axis=1, tiled=True),
        lax.all_to_all(spread_slots, "space", split_axis=1, concat_axis=1, tiled=True),
        lax.all_to_all(cell_slots, "space", split_axis=1, concat_axis=1, tiled=True),
    )
    present = got_cells[0] >= 0
    spot = jnp.maximum(got_cells[0], 0)
    flat = estimate.reshape(step_count * layer_count, row_count * col_count)
    seen = jnp.take(flat, spot, axis=1)
    misfit = jnp.where(
        present[None, :], (got_values - seen) / (got_spread + noise_scale * noise_scale), 0.0
    )
    pull = jnp.zeros_like(flat).at[:, spot].add(misfit)
    return (
        estimate
        + noise_scale * noise_scale * pull.reshape(estimate.shape)
        + next_scale * fresh_noise
    )


def solution(mesh):
    placed = (
        P("tm", None, "space", None),
        P("tm", None, "space", None),
        P(),
        P("tm", None, "space"),
        P("space"),
        P("space", None),
        P("space"),
        P(),
        P(),
        P(),
        P(),
        P(),
        P(),
        P(),
    )
    return jax.shard_map(
        local, mesh=mesh, in_specs=placed, out_specs=P("tm", None, "space", None), check_vma=False
    )
```

profile of v0, /device:TPU:0, one launch (start us, length us, event | category | flops | bytes accessed | tf_op | source)
XLA Modules:
  0.0 83.0 jit_solution(5439972341782676317)
XLA Ops:
  0.8 0.9 %divide_convert_fusion = bf16[4,2,16,256]{3,2,1,0:T(8,128)(2,1)S(1)} fusion(f32[4,2,16,256]{3,2,1,0:T(8,128)} %param.14, f32[]{:T(128)S(6)} %sqrt.3), kind=kLoop, calls=%fused_computation.84 | loop fusion | flops 65536 | bytes 196612 | tf_op jit(solution)/shard_map/convert_element_type | solution.py:94
  1.7 1.3 %collective-permute-start = (bf16[4,2,16,256]{3,2,1,0:T(8,128)(2,1)S(1)}, bf16[4,2,16,256]{3,2,1,0:T(8,128)(2,1)S(1)}, u32[]{:S(2)}, u32[]{:S(2)}) collective-permute-start(bf16[4,2,16,256]{3,2,1,0:T(8,128)(2,1)S(1)} %divide_convert_fusion), channel_id=1, source_target_pairs={{16,0},{17,1},{18,2},{19,3},{20,4},{21,5},{22,6},{23,7},{24,8},{25... | collective-permute-start | bytes 196616 | tf_op jit(solution)/shard_map/ppermute | solution.py:31
  3.0 0.8 select_reduce_fusion
  3.8 0.7 fusion.78
  4.5 1.1 %scatter_custom_fusion = s32[512]{0:T(512)S(1)} fusion(s32[128]{0:T(128)S(1)} %fusion.78, s32[128]{0:T(128)} %param.20, s32[]{:T(128)} %constant.78.clone.1), kind=kCustom, calls=%fused_computation.129 | custom fusion | bytes 2560 | tf_op jit(solution)/shard_map/scatter | solution.py:137
  5.6 0.7 all_to_all.20
  6.3 7.4 %all-to-all-start = ((s32[1,16,32]{2,0,1:T(1,128)}), s32[1,16,32]{2,0,1:T(1,128)S(1)}, u32[]{:S(2)}, u32[]{:S(2)}) async-start(s32[1,16,32]{2,0,1:T(1,128)} %all_to_all.20), calls=%async_computation | async-start | bytes 16384 | tf_op jit(solution)/shard_map/all_to_all | solution.py:141
  13.8 0.5 collective-permute-start.1
  14.3 0.7 multiply_add_fusion.1
  14.9 4.1 %collective-permute-start.2 = (bf16[1,16,1,256]{3,1,2,0:T(8,128)(2,1)S(1)}, bf16[1,16,1,256]{3,1,2,0:T(8,128)(2,1)S(1)}, u32[]{:S(2)}, u32[]{:S(2)}) collective-permute-start(bf16[1,16,1,256]{3,1,2,0:T(8,128)(2,1)S(1)} %copy.65), channel_id=1, source_target_pairs={{1,0},{2,1},{3,2},{4,3},{5,4},{6,5},{7,6},{8,7},{9,8},{10,9},{11,1... | collective-permute-start | bytes 24584 | tf_op jit(solution)/shard_map/ppermute | solution.py:21
  19.0 0.6 collective-permute-done.1
  19.7 0.7 collective-permute-done.2
  20.7 0.3 fusion.28
  21.1 0.3 convolution_add_fusion.1
  21.4 0.5 multiply_convert_fusion
  22.0 4.5 %collective-permute-start.4 = (bf16[1,64,1,256]{3,1,2,0:T(8,128)(2,1)S(1)}, bf16[1,64,1,256]{3,1,2,0:T(8,128)(2,1)S(1)}, u32[]{:S(2)}, u32[]{:S(2)}) collective-permute-start(bf16[1,64,1,256]{3,1,2,0:T(8,128)(2,1)S(1)} %get-tuple-element.24), channel_id=1, source_target_pairs={{1,0},{2,1},{3,2},{4,3},{5,4},{6,5},{7,6},{8,7},{9,8},{10,9},{11,1... | collective-permute-start | bytes 98312 | tf_op jit(solution)/shard_map/ppermute | solution.py:21
  26.5 1.1 %scatter_custom_fusion.2 = f32[512]{0:T(512)S(1)} fusion(s32[128]{0:T(128)S(1)} %fusion.78, f32[128]{0:T(128)} %param.18, f32[]{:T(128)} %constant.35.clone.1), kind=kCustom, calls=%fused_computation.127 | custom fusion | bytes 2560 | tf_op jit(solution)/shard_map/scatter | solution.py:136
  27.6 0.7 all_to_all.25
  28.4 0.9 %scatter_custom_fusion.1 = f32[8,512]{0,1:T(8,128)S(1)} fusion(s32[128]{0:T(128)S(1)} %fusion.78, f32[]{:T(128)} %constant.35.clone.1, f32[8,128]{0,1:T(8,128)S(1)} %copy.54), kind=kCustom, calls=%fused_computation.82 | custom fusion | bytes 81924 | tf_op jit(solution)/shard_map/scatter | solution.py:135
  29.5 0.7 reshape.297
  30.3 0.3 fusion.85
  30.8 1.4 %maximum_maximum_fusion = bf16[1,192,18,256]{3,1,2,0:T(8,128)(2,1)S(1)} fusion(bf16[1,64,18,1]{3,1,2,0:T(8,128)(2,1)S(1)} %get-tuple-element.16, bf16[1,64,18,255]{3,1,2,0:T(8,128)(2,1)S(1)} %get-tuple-element.18, bf16[1,64,1,256]{3,1,2,0:T(8,128)(2,1)S(1)} %collective-permute-done.4, bf16[1,64,16,256]{3,1,2,0:T(8,128)(2,1)S(1)} %multiply_convert_fusion, ...), kind=kLoop, calls=%fused_computation.5 | loop fusion | flops 12386304 | bytes 3538944 | tf_op jit(solution)/shard_map/concatenate | solution.py:40
  32.2 0.4 fusion.6
  32.6 0.4 fusion.7
  33.0 0.5 multiply_reduce_fusion
  33.7 0.4 fusion.27
  34.2 4.4 %collective-permute-start.6 = (bf16[1,64,1,256]{3,1,2,0:T(8,128)(2,1)S(1)}, bf16[1,64,1,256]{3,1,2,0:T(8,128)(2,1)S(1)}, u32[]{:S(2)}, u32[]{:S(2)}) collective-permute-start(bf16[1,64,1,256]{3,1,2,0:T(8,128)(2,1)S(1)} %get-tuple-element.22), channel_id=1, source_target_pairs={{1,0},{2,1},{3,2},{4,3},{5,4},{6,5},{7,6},{8,7},{9,8},{10,9},{11,1... | collective-permute-start | bytes 98312 | tf_op jit(solution)/shard_map/ppermute | solution.py:21
  38.6 3.4 %all-to-all-start.2 = ((f32[1,16,32]{2,0,1:T(1,128)}), f32[1,16,32]{2,0,1:T(1,128)S(1)}, u32[]{:S(2)}, u32[]{:S(2)}) async-start(f32[1,16,32]{2,0,1:T(1,128)} %all_to_all.25), calls=%async_computation.2 | async-start | bytes 16384 | tf_op jit(solution)/shard_map/all_to_all | solution.py:140
  42.7 1.4 %maximum_maximum_fusion.1 = bf16[1,192,18,256]{3,1,2,0:T(8,128)(2,1)S(1)} fusion(bf16[1,64,18,1]{3,1,2,0:T(8,128)(2,1)S(1)} %get-tuple-element.12, bf16[1,64,18,255]{3,1,2,0:T(8,128)(2,1)S(1)} %get-tuple-element.14, bf16[1,64,1,256]{3,1,2,0:T(8,128)(2,1)S(1)} %collective-permute-done.6, bf16[1,64,16,256]{3,1,2,0:T(8,128)(2,1)S(1)} %fusion.27, ...), kind=kLoop, calls=%fused_computation.6 | loop fusion | flops 12386304 | bytes 3538944 | tf_op jit(solution)/shard_map/concatenate | solution.py:40
  44.1 0.4 fusion.3
  44.5 0.4 fusion.4
  44.9 0.6 add_convert_fusion
  45.5 0.3 collective-permute-start.7
  45.9 4.2 %collective-permute-start.8 = (bf16[1,64,1,256]{3,1,2,0:T(8,128)(2,1)S(1)}, bf16[1,64,1,256]{3,1,2,0:T(8,128)(2,1)S(1)}, u32[]{:S(2)}, u32[]{:S(2)}) collective-permute-start(bf16[1,64,1,256]{3,1,2,0:T(8,128)(2,1)S(1)} %get-tuple-element.20), channel_id=1, source_target_pairs={{1,0},{2,1},{3,2},{4,3},{5,4},{6,5},{7,6},{8,7},{9,8},{10,9},{11,1... | collective-permute-start | bytes 98312 | tf_op jit(solution)/shard_map/ppermute | solution.py:21
  50.1 1.6 %collective-permute-done.7 = bf16[1,64,1,256]{3,1,2,0:T(8,128)(2,1)S(1)} collective-permute-done((bf16[1,64,1,256]{3,1,2,0:T(8,128)(2,1)S(1)}, bf16[1,64,1,256]{3,1,2,0:T(8,128)(2,1)S(1)}, u32[]{:S(2)}, u32[]{:S(2)}) %collective-permute-start.7) | collective-permute-done | bytes 32800 | tf_op jit(solution)/shard_map/ppermute | solution.py:19
  52.2 1.4 %maximum_maximum_fusion.2 = bf16[1,192,18,256]{3,1,2,0:T(8,128)(2,1)S(1)} fusion(bf16[1,64,18,1]{3,1,2,0:T(8,128)(2,1)S(1)} %get-tuple-element.8, bf16[1,64,18,255]{3,1,2,0:T(8,128)(2,1)S(1)} %get-tuple-element.10, bf16[1,64,1,256]{3,1,2,0:T(8,128)(2,1)S(1)} %collective-permute-done.8, bf16[1,64,16,256]{3,1,2,0:T(8,128)(2,1)S(1)} %add_convert_fusion, ...), kind=kLoop, calls=%fused_computation.7 | loop fusion | flops 12386304 | bytes 3538944 | tf_op jit(solution)/shard_map/concatenate | solution.py:40
  53.6 0.3 fusion
  53.9 0.3 fusion.1
  54.2 0.3 fusion.21
  54.8 4.5 %collective-permute-start.9 = (f32[4,2,16,256]{3,2,1,0:T(8,128)S(1)}, f32[4,2,16,256]{3,2,1,0:T(8,128)S(1)}, u32[]{:S(2)}, u32[]{:S(2)}) collective-permute-start(f32[4,2,16,256]{3,2,1,0:T(8,128)S(1)} %fusion.40), channel_id=1, source_target_pairs={{0,16},{1,17},{2,18},{3,19},{4,20},{5,21},{6,22},{7,23},{8,24},{9,... | collective-permute-start | bytes 393224 | tf_op jit(solution)/shard_map/ppermute | solution.py:31
  59.3 5.6 %all-to-all-start.1 = ((f32[16,1,256]{2,1,0:T(1,128)}), f32[16,1,256]{2,1,0:T(1,128)S(1)}, u32[]{:S(2)}, u32[]{:S(2)}) async-start(f32[16,1,256]{2,1,0:T(1,128)} %reshape.297), calls=%async_computation.1 | async-start | bytes 32768 | tf_op jit(solution)/shard_map/all_to_all | solution.py:139
  65.3 6.1 %all-to-all-done.1 = f32[16,1,256]{2,1,0:T(1,128)S(1)} async-done(((f32[16,1,256]{2,1,0:T(1,128)}), f32[16,1,256]{2,1,0:T(1,128)S(1)}, u32[]{:S(2)}, u32[]{:S(2)}) %all-to-all-start.1) | async-done | bytes 16416 | tf_op jit(solution)/shard_map/all_to_all | solution.py:139
  71.4 0.5 broadcast.170
  71.9 0.7 reduce.14
  73.0 0.6 copy.57
  73.6 6.4 %scatter_custom_fusion.3 = f32[8,4096]{0,1:T(8,128)} fusion(s32[512]{0:T(512)S(1)} %reshape.243, f32[]{:T(128)} %constant.35.clone.1, f32[8,512]{0,1:T(8,128)S(1)} %bitcast.203, f32[]{:T(128)} %constant.83.clone.1, f32[512]{0:T(512)S(1)} %add.188, pred[512]{0:T(512)(128)(4,1)S(1)} %le.21, pred[512]{0:T(512)(128)(4,1)S(1)} %ge.31, f32[8,4096]{0,1:T(8,128)S(1)} %copy.57, ...), kind=kCustom, calls=%fused_computation.46 | custom fusion | flops 20480 | bytes 2499072 | tf_op jit(solution)/shard_map/scatter-add | solution.py:150
  80.0 2.2 %copy.58 = f32[8,4096]{1,0:T(8,128)S(1)} copy(f32[8,4096]{0,1:T(8,128)} %scatter_custom_fusion.3) | data formatting | bytes 262144 | tf_op jit(solution)/shard_map/scatter-add | solution.py:150
  82.3 0.7 multiply_add_fusion
  (69 shorter events, 3.5 us)
Async XLA Ops:
  0.0 20.7 %copy-start.5 = (bf16[3,64,48]{1,2,0:T(8,128)(2,1)S(1)}, bf16[3,64,48]{1,2,0:T(8,128)(2,1)}, u32[]{:S(2)}) copy-start(bf16[3,64,48]{1,2,0:T(8,128)(2,1)} %param.21) | copy-start | bytes 55300
  1.7 12.0 %collective-permute-start = (bf16[4,2,16,256]{3,2,1,0:T(8,128)(2,1)S(1)}, bf16[4,2,16,256]{3,2,1,0:T(8,128)(2,1)S(1)}, u32[]{:S(2)}, u32[]{:S(2)}) collective-permute-start(bf16[4,2,16,256]{3,2,1,0:T(8,128)(2,1)S(1)} %divide_convert_fusion), channel_id=1, source_target_pairs={{16,0},{17,1},{18,2},{19,3},{20,4},{21,5},{22,6},{23,7},{24,8},{25... | collective-permute-start | bytes 196616 | tf_op jit(solution)/shard_map/ppermute | solution.py:31
  6.3 32.3 %all-to-all-start = ((s32[1,16,32]{2,0,1:T(1,128)}), s32[1,16,32]{2,0,1:T(1,128)S(1)}, u32[]{:S(2)}, u32[]{:S(2)}) async-start(s32[1,16,32]{2,0,1:T(1,128)} %all_to_all.20), calls=%async_computation | async-start | bytes 16384 | tf_op jit(solution)/shard_map/all_to_all | solution.py:141
  13.8 5.8 %collective-permute-start.1 = (bf16[1,16,1,256]{3,1,2,0:T(8,128)(2,1)S(1)}, bf16[1,16,1,256]{3,1,2,0:T(8,128)(2,1)S(1)}, u32[]{:S(2)}, u32[]{:S(2)}) collective-permute-start(bf16[1,16,1,256]{3,1,2,0:T(8,128)(2,1)S(1)} %copy.64), channel_id=1, source_target_pairs={{0,1},{1,2},{2,3},{3,4},{4,5},{5,6},{6,7},{7,8},{8,9},{9,10},{10,1... | collective-permute-start | bytes 24584 | tf_op jit(solution)/shard_map/ppermute | solution.py:19
  14.9 5.4 %collective-permute-start.2 = (bf16[1,16,1,256]{3,1,2,0:T(8,128)(2,1)S(1)}, bf16[1,16,1,256]{3,1,2,0:T(8,128)(2,1)S(1)}, u32[]{:S(2)}, u32[]{:S(2)}) collective-permute-start(bf16[1,16,1,256]{3,1,2,0:T(8,128)(2,1)S(1)} %copy.65), channel_id=1, source_target_pairs={{1,0},{2,1},{3,2},{4,3},{5,4},{6,5},{7,6},{8,7},{9,8},{10,9},{11,1... | collective-permute-start | bytes 24584 | tf_op jit(solution)/shard_map/ppermute | solution.py:21
  21.4 6.9 %copy-start.6 = (f32[4,2,128]{2,1,0:T(2,128)S(1)}, f32[4,2,128]{2,1,0:T(2,128)}, u32[]{:S(2)}) copy-start(f32[4,2,128]{2,1,0:T(2,128)} %param.17) | copy-start | bytes 12292
  22.0 8.3 %collective-permute-start.3 = (bf16[1,64,1,256]{3,1,2,0:T(8,128)(2,1)S(1)}, bf16[1,64,1,256]{3,1,2,0:T(8,128)(2,1)S(1)}, u32[]{:S(2)}, u32[]{:S(2)}) collective-permute-start(bf16[1,64,1,256]{3,1,2,0:T(8,128)(2,1)S(1)} %get-tuple-element.23), channel_id=1, source_target_pairs={{0,1},{1,2},{2,3},{3,4},{4,5},{5,6},{6,7},{7,8},{8,9},{9,10},{10,1... | collective-permute-start | bytes 98312 | tf_op jit(solution)/shard_map/ppermute | solution.py:19
  22.0 8.2 %collective-permute-start.4 = (bf16[1,64,1,256]{3,1,2,0:T(8,128)(2,1)S(1)}, bf16[1,64,1,256]{3,1,2,0:T(8,128)(2,1)S(1)}, u32[]{:S(2)}, u32[]{:S(2)}) collective-permute-start(bf16[1,64,1,256]{3,1,2,0:T(8,128)(2,1)S(1)} %get-tuple-element.24), channel_id=1, source_target_pairs={{1,0},{2,1},{3,2},{4,3},{5,4},{6,5},{7,6},{8,7},{9,8},{10,9},{11,1... | collective-permute-start | bytes 98312 | tf_op jit(solution)/shard_map/ppermute | solution.py:21
  30.8 1.4 %copy-start.2 = (bf16[3,64,192]{2,1,0:T(8,128)(2,1)S(1)}, bf16[3,64,192]{2,1,0:T(8,128)(2,1)}, u32[]{:S(2)}) copy-start(bf16[3,64,192]{2,1,0:T(8,128)(2,1)} %param.22) | copy-start | bytes 221188
  33.0 0.7 copy-start.7
  34.1 8.0 %collective-permute-start.5 = (bf16[1,64,1,256]{3,1,2,0:T(8,128)(2,1)S(1)}, bf16[1,64,1,256]{3,1,2,0:T(8,128)(2,1)S(1)}, u32[]{:S(2)}, u32[]{:S(2)}) collective-permute-start(bf16[1,64,1,256]{3,1,2,0:T(8,128)(2,1)S(1)} %get-tuple-element.21), channel_id=1, source_target_pairs={{0,1},{1,2},{2,3},{3,4},{4,5},{5,6},{6,7},{7,8},{8,9},{9,10},{10,1... | collective-permute-start | bytes 98312 | tf_op jit(solution)/shard_map/ppermute | solution.py:19
  34.2 8.0 %collective-permute-start.6 = (bf16[1,64,1,256]{3,1,2,0:T(8,128)(2,1)S(1)}, bf16[1,64,1,256]{3,1,2,0:T(8,128)(2,1)S(1)}, u32[]{:S(2)}, u32[]{:S(2)}) collective-permute-start(bf16[1,64,1,256]{3,1,2,0:T(8,128)(2,1)S(1)} %get-tuple-element.22), channel_id=1, source_target_pairs={{1,0},{2,1},{3,2},{4,3},{5,4},{6,5},{7,6},{8,7},{9,8},{10,9},{11,1... | collective-permute-start | bytes 98312 | tf_op jit(solution)/shard_map/ppermute | solution.py:21
  38.6 20.7 %all-to-all-start.2 = ((f32[1,16,32]{2,0,1:T(1,128)}), f32[1,16,32]{2,0,1:T(1,128)S(1)}, u32[]{:S(2)}, u32[]{:S(2)}) async-start(f32[1,16,32]{2,0,1:T(1,128)} %all_to_all.25), calls=%async_computation.2 | async-start | bytes 16384 | tf_op jit(solution)/shard_map/all_to_all | solution.py:140
  42.7 1.4 %copy-start.3 = (bf16[3,64,192]{2,1,0:T(8,128)(2,1)S(1)}, bf16[3,64,192]{2,1,0:T(8,128)(2,1)}, u32[]{:S(2)}) copy-start(bf16[3,64,192]{2,1,0:T(8,128)(2,1)} %param.23) | copy-start | bytes 221188
  45.5 6.1 %collective-permute-start.7 = (bf16[1,64,1,256]{3,1,2,0:T(8,128)(2,1)S(1)}, bf16[1,64,1,256]{3,1,2,0:T(8,128)(2,1)S(1)}, u32[]{:S(2)}, u32[]{:S(2)}) collective-permute-start(bf16[1,64,1,256]{3,1,2,0:T(8,128)(2,1)S(1)} %get-tuple-element.19), channel_id=1, source_target_pairs={{0,1},{1,2},{2,3},{3,4},{4,5},{5,6},{6,7},{7,8},{8,9},{9,10},{10,1... | collective-permute-start | bytes 98312 | tf_op jit(solution)/shard_map/ppermute | solution.py:19
  45.9 5.8 %collective-permute-start.8 = (bf16[1,64,1,256]{3,1,2,0:T(8,128)(2,1)S(1)}, bf16[1,64,1,256]{3,1,2,0:T(8,128)(2,1)S(1)}, u32[]{:S(2)}, u32[]{:S(2)}) collective-permute-start(bf16[1,64,1,256]{3,1,2,0:T(8,128)(2,1)S(1)} %get-tuple-element.20), channel_id=1, source_target_pairs={{1,0},{2,1},{3,2},{4,3},{5,4},{6,5},{7,6},{8,7},{9,8},{10,9},{11,1... | collective-permute-start | bytes 98312 | tf_op jit(solution)/shard_map/ppermute | solution.py:21
  52.2 1.4 %copy-start.4 = (bf16[3,16,192]{2,1,0:T(8,128)(2,1)S(1)}, bf16[3,16,192]{2,1,0:T(8,128)(2,1)}, u32[]{:S(2)}) copy-start(bf16[3,16,192]{2,1,0:T(8,128)(2,1)} %param.24) | copy-start | bytes 55300
  54.2 18.6 %copy-start = (f32[4,2,16,256]{3,2,1,0:T(8,128)S(1)}, f32[4,2,16,256]{3,2,1,0:T(8,128)}, u32[]{:S(2)}) copy-start(f32[4,2,16,256]{3,2,1,0:T(8,128)} %param.14) | copy-start | bytes 393220
  54.8 18.0 %collective-permute-start.9 = (f32[4,2,16,256]{3,2,1,0:T(8,128)S(1)}, f32[4,2,16,256]{3,2,1,0:T(8,128)S(1)}, u32[]{:S(2)}, u32[]{:S(2)}) collective-permute-start(f32[4,2,16,256]{3,2,1,0:T(8,128)S(1)} %fusion.40), channel_id=1, source_target_pairs={{0,16},{1,17},{2,18},{3,19},{4,20},{5,21},{6,22},{7,23},{8,24},{9,... | collective-permute-start | bytes 393224 | tf_op jit(solution)/shard_map/ppermute | solution.py:31
  59.3 12.1 %all-to-all-start.1 = ((f32[16,1,256]{2,1,0:T(1,128)}), f32[16,1,256]{2,1,0:T(1,128)S(1)}, u32[]{:S(2)}, u32[]{:S(2)}) async-start(f32[16,1,256]{2,1,0:T(1,128)} %reshape.297), calls=%async_computation.1 | async-start | bytes 32768 | tf_op jit(solution)/shard_map/all_to_all | solution.py:139
  80.0 2.3 %copy-start.1 = (f32[4,2,16,256]{3,2,1,0:T(8,128)S(1)}, f32[4,2,16,256]{3,2,1,0:T(8,128)}, u32[]{:S(2)}) copy-start(f32[4,2,16,256]{3,2,1,0:T(8,128)} %param.15) | copy-start | bytes 393220
where the time goes:
time: 83.5 us; the launch traced here: 83 us
  starting transfers between devices  40.3 us (48%)
  other arithmetic  16 us (19%)
  local copies, waits for them, and re-layouts  11.5 us (14%)
  waiting for transfers between devices  9.03 us (11%)
  matrix products  4.83 us (6%)
  between operations  1.38 us (2%)
    ppermute x4, starting transfers between devices, extended_2(): lax.ppermute(head, axis, [((i + 1) % count, i) for i in range(count)])  17.1 us
    all_to_all x1, starting transfers between devices, local(): lax.all_to_all(cell_slots, 'space', split_axis=1, concat_axis=1, tiled=True)  7.39 us
    scatter-add x1, other arithmetic, local(): pull = jnp.zeros_like(flat).at[:, spot].add(misfit)  6.41 us
    all_to_all x1, waiting for transfers between devices, local(): lax.all_to_all(value_slots, 'space', split_axis=1, concat_axis=1, tiled=T...  6.12 us
    ppermute x2, starting transfers between devices, shifted(): lax.ppermute(value, axis, [(source, source + steps) for source in range(f...  5.84 us
    all_to_all x1, starting transfers between devices, local(): lax.all_to_all(value_slots, 'space', split_axis=1, concat_axis=1, tiled=T...  5.56 us
    dot_general x12, matrix products, conv_rows(): jnp.einsum('oc,ncyx->noyx', weight[row_tap], stacked[:, :, row_tap:row_ta...  4.83 us
    concatenate x4, other arithmetic, conv_rows(): jnp.concatenate([jnp.roll(padded, 1 - col_tap, axis=3) for col_tap in ran...  4.2 us
  transfers between devices with their start and end apart: 13, of which 4 were waited for; matrix products, arithmetic and copies ran while one was open for 24% of the time, Pallas kernels for 0%

commit v1 on v0

--- a/solution.py
+++ b/solution.py
@@ -7,6 +7,13 @@
 LEVELS = 32
 STRIDE = 4
 CHAN = 16
+
+
+def stacked_exchange(x, name, split, join):
+    devices = lax.axis_size(name)
+    parts = jnp.stack(jnp.split(x, devices, axis=split), axis=0)
+    parts = lax.all_to_all(parts, name, split_axis=0, concat_axis=0)
+    return jnp.concatenate(parts, axis=join)
 
 
 def extended_2(cells, sides, width):
@@ -138,7 +145,7 @@
     got_values, got_spread, got_cells = (
         lax.all_to_all(value_slots, "space", split_axis=1, concat_axis=1, tiled=True),
         lax.all_to_all(spread_slots, "space", split_axis=1, concat_axis=1, tiled=True),
-        lax.all_to_all(cell_slots, "space", split_axis=1, concat_axis=1, tiled=True),
+        stacked_exchange(cell_slots, "space", 1, 1),
     )
     present = got_cells[0] >= 0
     spot = jnp.maximum(got_cells[0], 0)

time: 83.5 us -> 92.4 us (1.11)
  local copies, waits for them, and re-layouts: 11.5 us -> 20.4 us
    unnamed x24 -> x39, local copies, waits for them, and re-layouts: 1.17 us -> 10.1 us
  transfers between devices with their start and end apart: 13 -> 13, of which waited for: 4 -> 4; matrix products, arithmetic and copies ran while one was open for 24% -> 32% of each run, Pallas kernels for 0% -> 0%
where the time goes in v1:
time: 92.4 us; the launch traced here: 92 us
  starting transfers between devices  40.3 us (44%)
  local copies, waits for them, and re-layouts  20.4 us (22%)
  other arithmetic  16 us (17%)
  waiting for transfers between devices  9.03 us (10%)
  matrix products  4.82 us (5%)
  between operations  1.39 us (2%)
    ppermute x4, starting transfers between devices, extended_2(): lax.ppermute(head, axis, [((i + 1) % count, i) for i in range(count)])  17.1 us
    unnamed x39, local copies, waits for them, and re-layouts  10.1 us
    all_to_all x1, starting transfers between devices, stacked_exchange(): parts = lax.all_to_all(parts, name, split_axis=0, concat_axis=0)  7.39 us
    scatter-add x1, other arithmetic, local(): pull = jnp.zeros_like(flat).at[:, spot].add(misfit)  6.41 us
    all_to_all x1, waiting for transfers between devices, local(): lax.all_to_all(value_slots, 'space', split_axis=1, concat_axis=1, tiled=T...  6.12 us
    ppermute x2, starting transfers between devices, shifted(): lax.ppermute(value, axis, [(source, source + steps) for source in range(f...  5.84 us
    all_to_all x1, starting transfers between devices, local(): lax.all_to_all(value_slots, 'space', split_axis=1, concat_axis=1, tiled=T...  5.56 us
    dot_general x12, matrix products, conv_rows(): jnp.einsum('oc,ncyx->noyx', weight[row_tap], stacked[:, :, row_tap:row_ta...  4.82 us
  transfers between devices with their start and end apart: 13, of which 4 were waited for; matrix products, arithmetic and copies ran while one was open for 32% of the time, Pallas kernels for 0%

profile of v1, /device:TPU:0, one launch (start us, length us, event | category | flops | bytes accessed | tf_op | source)
XLA Modules:
  0.0 92.0 jit_solution(17451010230379906396)
XLA Ops:
  0.8 0.9 %divide_convert_fusion = bf16[4,2,16,256]{3,2,1,0:T(8,128)(2,1)S(1)} fusion(f32[4,2,16,256]{3,2,1,0:T(8,128)} %param.14, f32[]{:T(128)S(6)} %sqrt.3), kind=kLoop, calls=%fused_computation.84 | loop fusion | flops 65536 | bytes 196612 | tf_op jit(solution)/shard_map/convert_element_type | solution.py:101
  1.7 1.3 %collective-permute-start = (bf16[4,2,16,256]{3,2,1,0:T(8,128)(2,1)S(1)}, bf16[4,2,16,256]{3,2,1,0:T(8,128)(2,1)S(1)}, u32[]{:S(2)}, u32[]{:S(2)}) collective-permute-start(bf16[4,2,16,256]{3,2,1,0:T(8,128)(2,1)S(1)} %divide_convert_fusion), channel_id=1, source_target_pairs={{16,0},{17,1},{18,2},{19,3},{20,4},{21,5},{22,6},{23,7},{24,8},{25... | collective-permute-start | bytes 196616 | tf_op jit(solution)/shard_map/ppermute | solution.py:38
  3.0 0.8 select_reduce_fusion
  3.8 0.7 fusion.78
  4.5 1.1 %scatter_custom_fusion = s32[512]{0:T(512)S(1)} fusion(s32[128]{0:T(128)S(1)} %fusion.78, s32[128]{0:T(128)} %param.20, s32[]{:T(128)} %constant.78.clone.1), kind=kCustom, calls=%fused_computation.145 | custom fusion | bytes 2560 | tf_op jit(solution)/shard_map/scatter | solution.py:144
  5.6 0.5 constant_dynamic-update-slice_fusion.18
  6.1 0.6 constant_dynamic-update-slice_fusion.17
  6.7 0.6 constant_dynamic-update-slice_fusion.16
  7.4 0.6 constant_dynamic-update-slice_fusion.15
  8.0 0.6 constant_dynamic-update-slice_fusion.14
  8.6 0.6 constant_dynamic-update-slice_fusion.13
  9.2 0.6 constant_dynamic-update-slice_fusion.12
  9.7 0.7 constant_dynamic-update-slice_fusion.11
  10.4 0.6 constant_dynamic-update-slice_fusion.10
  11.0 0.6 constant_dynamic-update-slice_fusion.9
  11.5 0.6 constant_dynamic-update-slice_fusion.8
  12.1 0.6 constant_dynamic-update-slice_fusion.7
  13.2 0.6 constant_dynamic-update-slice_fusion.5
  13.9 0.7 constant_dynamic-update-slice_fusion.4
  14.5 0.6 constant_dynamic-update-slice_fusion.3
  15.2 7.4 %all-to-all-start = ((s32[16,1,32]{2,1,0:T(1,128)}), s32[16,1,32]{2,1,0:T(1,128)S(1)}, u32[]{:S(2)}, u32[]{:S(2)}) async-start(s32[16,1,32]{2,1,0:T(1,128)} %constant_dynamic-update-slice_fusion.3), calls=%async_computation | async-start | bytes 16384 | tf_op jit(solution)/shard_map/all_to_all | solution.py:15
  23.2 0.7 multiply_add_fusion.1
  23.9 4.1 %collective-permute-start.2 = (bf16[1,16,1,256]{3,1,2,0:T(8,128)(2,1)S(1)}, bf16[1,16,1,256]{3,1,2,0:T(8,128)(2,1)S(1)}, u32[]{:S(2)}, u32[]{:S(2)}) collective-permute-start(bf16[1,16,1,256]{3,1,2,0:T(8,128)(2,1)S(1)} %copy.57), channel_id=1, source_target_pairs={{1,0},{2,1},{3,2},{4,3},{5,4},{6,5},{7,6},{8,7},{9,8},{10,9},{11,1... | collective-permute-start | bytes 24584 | tf_op jit(solution)/shard_map/ppermute | solution.py:28
  27.9 0.6 collective-permute-done.1
  28.6 0.7 collective-permute-done.2
  30.4 0.5 multiply_convert_fusion
  30.9 4.5 %collective-permute-start.4 = (bf16[1,64,1,256]{3,1,2,0:T(8,128)(2,1)S(1)}, bf16[1,64,1,256]{3,1,2,0:T(8,128)(2,1)S(1)}, u32[]{:S(2)}, u32[]{:S(2)}) collective-permute-start(bf16[1,64,1,256]{3,1,2,0:T(8,128)(2,1)S(1)} %get-tuple-element.24), channel_id=1, source_target_pairs={{1,0},{2,1},{3,2},{4,3},{5,4},{6,5},{7,6},{8,7},{9,8},{10,9},{11,1... | collective-permute-start | bytes 98312 | tf_op jit(solution)/shard_map/ppermute | solution.py:28
  35.4 1.1 %scatter_custom_fusion.2 = f32[512]{0:T(512)S(1)} fusion(s32[128]{0:T(128)S(1)} %fusion.78, f32[128]{0:T(128)} %param.18, f32[]{:T(128)} %constant.35.clone.1), kind=kCustom, calls=%fused_computation.143 | custom fusion | bytes 2560 | tf_op jit(solution)/shard_map/scatter | solution.py:143
  36.5 0.7 all_to_all.21
  37.3 0.9 %scatter_custom_fusion.1 = f32[8,512]{0,1:T(8,128)S(1)} fusion(s32[128]{0:T(128)S(1)} %fusion.78, f32[]{:T(128)} %constant.35.clone.1, f32[8,128]{0,1:T(8,128)S(1)} %copy.46), kind=kCustom, calls=%fused_computation.82 | custom fusion | bytes 81924 | tf_op jit(solution)/shard_map/scatter | solution.py:142
  38.4 0.7 reshape.293
  39.8 1.4 %maximum_maximum_fusion = bf16[1,192,18,256]{3,1,2,0:T(8,128)(2,1)S(1)} fusion(bf16[1,64,18,1]{3,1,2,0:T(8,128)(2,1)S(1)} %get-tuple-element.16, bf16[1,64,18,255]{3,1,2,0:T(8,128)(2,1)S(1)} %get-tuple-element.18, bf16[1,64,1,256]{3,1,2,0:T(8,128)(2,1)S(1)} %collective-permute-done.4, bf16[1,64,16,256]{3,1,2,0:T(8,128)(2,1)S(1)} %multiply_convert_fusion, ...), kind=kLoop, calls=%fused_computation.5 | loop fusion | flops 12386304 | bytes 3538944 | tf_op jit(solution)/shard_map/concatenate | solution.py:47
  43.1 4.4 %collective-permute-start.6 = (bf16[1,64,1,256]{3,1,2,0:T(8,128)(2,1)S(1)}, bf16[1,64,1,256]{3,1,2,0:T(8,128)(2,1)S(1)}, u32[]{:S(2)}, u32[]{:S(2)}) collective-permute-start(bf16[1,64,1,256]{3,1,2,0:T(8,128)(2,1)S(1)} %get-tuple-element.22), channel_id=1, source_target_pairs={{1,0},{2,1},{3,2},{4,3},{5,4},{6,5},{7,6},{8,7},{9,8},{10,9},{11,1... | collective-permute-start | bytes 98312 | tf_op jit(solution)/shard_map/ppermute | solution.py:28
  47.5 3.5 %all-to-all-start.2 = ((f32[1,16,32]{2,0,1:T(1,128)}), f32[1,16,32]{2,0,1:T(1,128)S(1)}, u32[]{:S(2)}, u32[]{:S(2)}) async-start(f32[1,16,32]{2,0,1:T(1,128)} %all_to_all.21), calls=%async_computation.2 | async-start | bytes 16384 | tf_op jit(solution)/shard_map/all_to_all | solution.py:147
  51.7 1.4 %maximum_maximum_fusion.1 = bf16[1,192,18,256]{3,1,2,0:T(8,128)(2,1)S(1)} fusion(bf16[1,64,18,1]{3,1,2,0:T(8,128)(2,1)S(1)} %get-tuple-element.12, bf16[1,64,18,255]{3,1,2,0:T(8,128)(2,1)S(1)} %get-tuple-element.14, bf16[1,64,1,256]{3,1,2,0:T(8,128)(2,1)S(1)} %collective-permute-done.6, bf16[1,64,16,256]{3,1,2,0:T(8,128)(2,1)S(1)} %fusion.27, ...), kind=kLoop, calls=%fused_computation.6 | loop fusion | flops 12386304 | bytes 3538944 | tf_op jit(solution)/shard_map/concatenate | solution.py:47
  53.9 0.6 add_convert_fusion
  54.8 4.2 %collective-permute-start.8 = (bf16[1,64,1,256]{3,1,2,0:T(8,128)(2,1)S(1)}, bf16[1,64,1,256]{3,1,2,0:T(8,128)(2,1)S(1)}, u32[]{:S(2)}, u32[]{:S(2)}) collective-permute-start(bf16[1,64,1,256]{3,1,2,0:T(8,128)(2,1)S(1)} %get-tuple-element.20), channel_id=1, source_target_pairs={{1,0},{2,1},{3,2},{4,3},{5,4},{6,5},{7,6},{8,7},{9,8},{10,9},{11,1... | collective-permute-start | bytes 98312 | tf_op jit(solution)/shard_map/ppermute | solution.py:28
  59.0 1.6 %collective-permute-done.7 = bf16[1,64,1,256]{3,1,2,0:T(8,128)(2,1)S(1)} collective-permute-done((bf16[1,64,1,256]{3,1,2,0:T(8,128)(2,1)S(1)}, bf16[1,64,1,256]{3,1,2,0:T(8,128)(2,1)S(1)}, u32[]{:S(2)}, u32[]{:S(2)}) %collective-permute-start.7) | collective-permute-done | bytes 32800 | tf_op jit(solution)/shard_map/ppermute | solution.py:26
  61.2 1.4 %maximum_maximum_fusion.2 = bf16[1,192,18,256]{3,1,2,0:T(8,128)(2,1)S(1)} fusion(bf16[1,64,18,1]{3,1,2,0:T(8,128)(2,1)S(1)} %get-tuple-element.8, bf16[1,64,18,255]{3,1,2,0:T(8,128)(2,1)S(1)} %get-tuple-element.10, bf16[1,64,1,256]{3,1,2,0:T(8,128)(2,1)S(1)} %collective-permute-done.8, bf16[1,64,16,256]{3,1,2,0:T(8,128)(2,1)S(1)} %add_convert_fusion, ...), kind=kLoop, calls=%fused_computation.7 | loop fusion | flops 12386304 | bytes 3538944 | tf_op jit(solution)/shard_map/concatenate | solution.py:47
  63.7 4.5 %collective-permute-start.9 = (f32[4,2,16,256]{3,2,1,0:T(8,128)S(1)}, f32[4,2,16,256]{3,2,1,0:T(8,128)S(1)}, u32[]{:S(2)}, u32[]{:S(2)}) collective-permute-start(f32[4,2,16,256]{3,2,1,0:T(8,128)S(1)} %fusion.40), channel_id=1, source_target_pairs={{0,16},{1,17},{2,18},{3,19},{4,20},{5,21},{6,22},{7,23},{8,24},{9,... | collective-permute-start | bytes 393224 | tf_op jit(solution)/shard_map/ppermute | solution.py:38
  68.3 5.6 %all-to-all-start.1 = ((f32[16,1,256]{2,1,0:T(1,128)}), f32[16,1,256]{2,1,0:T(1,128)S(1)}, u32[]{:S(2)}, u32[]{:S(2)}) async-start(f32[16,1,256]{2,1,0:T(1,128)} %reshape.293), calls=%async_computation.1 | async-start | bytes 32768 | tf_op jit(solution)/shard_map/all_to_all | solution.py:146
  74.2 6.1 %all-to-all-done.1 = f32[16,1,256]{2,1,0:T(1,128)S(1)} async-done(((f32[16,1,256]{2,1,0:T(1,128)}), f32[16,1,256]{2,1,0:T(1,128)S(1)}, u32[]{:S(2)}, u32[]{:S(2)}) %all-to-all-start.1) | async-done | bytes 16416 | tf_op jit(solution)/shard_map/all_to_all | solution.py:146
  80.3 0.5 broadcast.170
  80.9 0.7 reduce.14
  82.0 0.6 copy.49
  82.6 6.4 %scatter_custom_fusion.3 = f32[8,4096]{0,1:T(8,128)} fusion(s32[512]{0:T(512)S(1)} %reshape.240, f32[]{:T(128)} %constant.35.clone.1, f32[8,512]{0,1:T(8,128)S(1)} %bitcast.268, f32[]{:T(128)} %constant.83.clone.1, f32[512]{0:T(512)S(1)} %add.188, pred[512]{0:T(512)(128)(4,1)S(1)} %le.21, pred[512]{0:T(512)(128)(4,1)S(1)} %ge.31, f32[8,4096]{0,1:T(8,128)S(1)} %copy.49, ...), kind=kCustom, calls=%fused_computation.46 | custom fusion | flops 20480 | bytes 2499072 | tf_op jit(solution)/shard_map/scatter-add | solution.py:157
  89.0 2.2 %copy.50 = f32[8,4096]{1,0:T(8,128)S(1)} copy(f32[8,4096]{0,1:T(8,128)} %scatter_custom_fusion.3) | data formatting | bytes 262144 | tf_op jit(solution)/shard_map/scatter-add | solution.py:157
  91.3 0.7 multiply_add_fusion
  (84 shorter events, 9.2 us)
Async XLA Ops:
  0.0 29.6 %copy-start.5 = (bf16[3,64,48]{1,2,0:T(8,128)(2,1)S(1)}, bf16[3,64,48]{1,2,0:T(8,128)(2,1)}, u32[]{:S(2)}) copy-start(bf16[3,64,48]{1,2,0:T(8,128)(2,1)} %param.21) | copy-start | bytes 55300
  1.7 20.9 %collective-permute-start = (bf16[4,2,16,256]{3,2,1,0:T(8,128)(2,1)S(1)}, bf16[4,2,16,256]{3,2,1,0:T(8,128)(2,1)S(1)}, u32[]{:S(2)}, u32[]{:S(2)}) collective-permute-start(bf16[4,2,16,256]{3,2,1,0:T(8,128)(2,1)S(1)} %divide_convert_fusion), channel_id=1, source_target_pairs={{16,0},{17,1},{18,2},{19,3},{20,4},{21,5},{22,6},{23,7},{24,8},{25... | collective-permute-start | bytes 196616 | tf_op jit(solution)/shard_map/ppermute | solution.py:38
  15.2 32.3 %all-to-all-start = ((s32[16,1,32]{2,1,0:T(1,128)}), s32[16,1,32]{2,1,0:T(1,128)S(1)}, u32[]{:S(2)}, u32[]{:S(2)}) async-start(s32[16,1,32]{2,1,0:T(1,128)} %constant_dynamic-update-slice_fusion.3), calls=%async_computation | async-start | bytes 16384 | tf_op jit(solution)/shard_map/all_to_all | solution.py:15
  22.7 5.8 %collective-permute-start.1 = (bf16[1,16,1,256]{3,1,2,0:T(8,128)(2,1)S(1)}, bf16[1,16,1,256]{3,1,2,0:T(8,128)(2,1)S(1)}, u32[]{:S(2)}, u32[]{:S(2)}) collective-permute-start(bf16[1,16,1,256]{3,1,2,0:T(8,128)(2,1)S(1)} %copy.56), channel_id=1, source_target_pairs={{0,1},{1,2},{2,3},{3,4},{4,5},{5,6},{6,7},{7,8},{8,9},{9,10},{10,1... | collective-permute-start | bytes 24584 | tf_op jit(solution)/shard_map/ppermute | solution.py:26
  23.9 5.4 %collective-permute-start.2 = (bf16[1,16,1,256]{3,1,2,0:T(8,128)(2,1)S(1)}, bf16[1,16,1,256]{3,1,2,0:T(8,128)(2,1)S(1)}, u32[]{:S(2)}, u32[]{:S(2)}) collective-permute-start(bf16[1,16,1,256]{3,1,2,0:T(8,128)(2,1)S(1)} %copy.57), channel_id=1, source_target_pairs={{1,0},{2,1},{3,2},{4,3},{5,4},{6,5},{7,6},{8,7},{9,8},{10,9},{11,1... | collective-permute-start | bytes 24584 | tf_op jit(solution)/shard_map/ppermute | solution.py:28
  30.3 6.9 %copy-start.6 = (f32[4,2,128]{2,1,0:T(2,128)S(1)}, f32[4,2,128]{2,1,0:T(2,128)}, u32[]{:S(2)}) copy-start(f32[4,2,128]{2,1,0:T(2,128)} %param.17) | copy-start | bytes 12292
  30.9 8.3 %collective-permute-start.3 = (bf16[1,64,1,256]{3,1,2,0:T(8,128)(2,1)S(1)}, bf16[1,64,1,256]{3,1,2,0:T(8,128)(2,1)S(1)}, u32[]{:S(2)}, u32[]{:S(2)}) collective-permute-start(bf16[1,64,1,256]{3,1,2,0:T(8,128)(2,1)S(1)} %get-tuple-element.23), channel_id=1, source_target_pairs={{0,1},{1,2},{2,3},{3,4},{4,5},{5,6},{6,7},{7,8},{8,9},{9,10},{10,1... | collective-permute-start | bytes 98312 | tf_op jit(solution)/shard_map/ppermute | solution.py:26
  30.9 8.2 %collective-permute-start.4 = (bf16[1,64,1,256]{3,1,2,0:T(8,128)(2,1)S(1)}, bf16[1,64,1,256]{3,1,2,0:T(8,128)(2,1)S(1)}, u32[]{:S(2)}, u32[]{:S(2)}) collective-permute-start(bf16[1,64,1,256]{3,1,2,0:T(8,128)(2,1)S(1)} %get-tuple-element.24), channel_id=1, source_target_pairs={{1,0},{2,1},{3,2},{4,3},{5,4},{6,5},{7,6},{8,7},{9,8},{10,9},{11,1... | collective-permute-start | bytes 98312 | tf_op jit(solution)/shard_map/ppermute | solution.py:28
  39.7 1.4 %copy-start.2 = (bf16[3,64,192]{2,1,0:T(8,128)(2,1)S(1)}, bf16[3,64,192]{2,1,0:T(8,128)(2,1)}, u32[]{:S(2)}) copy-start(bf16[3,64,192]{2,1,0:T(8,128)(2,1)} %param.22) | copy-start | bytes 221188
  41.9 0.7 copy-start.7
  43.0 8.0 %collective-permute-start.5 = (bf16[1,64,1,256]{3,1,2,0:T(8,128)(2,1)S(1)}, bf16[1,64,1,256]{3,1,2,0:T(8,128)(2,1)S(1)}, u32[]{:S(2)}, u32[]{:S(2)}) collective-permute-start(bf16[1,64,1,256]{3,1,2,0:T(8,128)(2,1)S(1)} %get-tuple-element.21), channel_id=1, source_target_pairs={{0,1},{1,2},{2,3},{3,4},{4,5},{5,6},{6,7},{7,8},{8,9},{9,10},{10,1... | collective-permute-start | bytes 98312 | tf_op jit(solution)/shard_map/ppermute | solution.py:26
  43.1 8.0 %collective-permute-start.6 = (bf16[1,64,1,256]{3,1,2,0:T(8,128)(2,1)S(1)}, bf16[1,64,1,256]{3,1,2,0:T(8,128)(2,1)S(1)}, u32[]{:S(2)}, u32[]{:S(2)}) collective-permute-start(bf16[1,64,1,256]{3,1,2,0:T(8,128)(2,1)S(1)} %get-tuple-element.22), channel_id=1, source_target_pairs={{1,0},{2,1},{3,2},{4,3},{5,4},{6,5},{7,6},{8,7},{9,8},{10,9},{11,1... | collective-permute-start | bytes 98312 | tf_op jit(solution)/shard_map/ppermute | solution.py:28
  47.5 20.7 %all-to-all-start.2 = ((f32[1,16,32]{2,0,1:T(1,128)}), f32[1,16,32]{2,0,1:T(1,128)S(1)}, u32[]{:S(2)}, u32[]{:S(2)}) async-start(f32[1,16,32]{2,0,1:T(1,128)} %all_to_all.21), calls=%async_computation.2 | async-start | bytes 16384 | tf_op jit(solution)/shard_map/all_to_all | solution.py:147
  51.7 1.4 %copy-start.3 = (bf16[3,64,192]{2,1,0:T(8,128)(2,1)S(1)}, bf16[3,64,192]{2,1,0:T(8,128)(2,1)}, u32[]{:S(2)}) copy-start(bf16[3,64,192]{2,1,0:T(8,128)(2,1)} %param.23) | copy-start | bytes 221188
  54.5 6.1 %collective-permute-start.7 = (bf16[1,64,1,256]{3,1,2,0:T(8,128)(2,1)S(1)}, bf16[1,64,1,256]{3,1,2,0:T(8,128)(2,1)S(1)}, u32[]{:S(2)}, u32[]{:S(2)}) collective-permute-start(bf16[1,64,1,256]{3,1,2,0:T(8,128)(2,1)S(1)} %get-tuple-element.19), channel_id=1, source_target_pairs={{0,1},{1,2},{2,3},{3,4},{4,5},{5,6},{6,7},{7,8},{8,9},{9,10},{10,1... | collective-permute-start | bytes 98312 | tf_op jit(solution)/shard_map/ppermute | solution.py:26
  54.8 5.8 %collective-permute-start.8 = (bf16[1,64,1,256]{3,1,2,0:T(8,128)(2,1)S(1)}, bf16[1,64,1,256]{3,1,2,0:T(8,128)(2,1)S(1)}, u32[]{:S(2)}, u32[]{:S(2)}) collective-permute-start(bf16[1,64,1,256]{3,1,2,0:T(8,128)(2,1)S(1)} %get-tuple-element.20), channel_id=1, source_target_pairs={{1,0},{2,1},{3,2},{4,3},{5,4},{6,5},{7,6},{8,7},{9,8},{10,9},{11,1... | collective-permute-start | bytes 98312 | tf_op jit(solution)/shard_map/ppermute | solution.py:28
  61.1 1.4 %copy-start.4 = (bf16[3,16,192]{2,1,0:T(8,128)(2,1)S(1)}, bf16[3,16,192]{2,1,0:T(8,128)(2,1)}, u32[]{:S(2)}) copy-start(bf16[3,16,192]{2,1,0:T(8,128)(2,1)} %param.24) | copy-start | bytes 55300
  63.2 18.6 %copy-start = (f32[4,2,16,256]{3,2,1,0:T(8,128)S(1)}, f32[4,2,16,256]{3,2,1,0:T(8,128)}, u32[]{:S(2)}) copy-start(f32[4,2,16,256]{3,2,1,0:T(8,128)} %param.14) | copy-start | bytes 393220
  63.7 18.0 %collective-permute-start.9 = (f32[4,2,16,256]{3,2,1,0:T(8,128)S(1)}, f32[4,2,16,256]{3,2,1,0:T(8,128)S(1)}, u32[]{:S(2)}, u32[]{:S(2)}) collective-permute-start(f32[4,2,16,256]{3,2,1,0:T(8,128)S(1)} %fusion.40), channel_id=1, source_target_pairs={{0,16},{1,17},{2,18},{3,19},{4,20},{5,21},{6,22},{7,23},{8,24},{9,... | collective-permute-start | bytes 393224 | tf_op jit(solution)/shard_map/ppermute | solution.py:38
  68.3 12.1 %all-to-all-start.1 = ((f32[16,1,256]{2,1,0:T(1,128)}), f32[16,1,256]{2,1,0:T(1,128)S(1)}, u32[]{:S(2)}, u32[]{:S(2)}) async-start(f32[16,1,256]{2,1,0:T(1,128)} %reshape.293), calls=%async_computation.1 | async-start | bytes 32768 | tf_op jit(solution)/shard_map/all_to_all | solution.py:146
  89.0 2.3 %copy-start.1 = (f32[4,2,16,256]{3,2,1,0:T(8,128)S(1)}, f32[4,2,16,256]{3,2,1,0:T(8,128)}, u32[]{:S(2)}) copy-start(f32[4,2,16,256]{3,2,1,0:T(8,128)} %param.15) | copy-start | bytes 393220
